TPU v7x, 512 devices: a whole 4x4x16 slice. The times are simulated.
512 devices in a mesh: seq: 64 (over z, x_lo, core), fsdp: 8 (over y, x_hi).
Axes of the slice: x: 4 (x_hi: 2, x_lo: 2; x = x_hi * 2 + x_lo), y: 4, z: 16, core: 2. Of those that a mesh axis runs over, the one named last changes fastest.
Arguments:
- q_s: bfloat16 [8, 64, 128, 1536], P('fsdp', 'seq'), may hold values from -48 to 48, as said below
- k_s: bfloat16 [8, 64, 128, 1536], P('fsdp', 'seq'), may hold values from -6 to 6, as said below
- v_s: bfloat16 [8, 64, 128, 1536], P('fsdp', 'seq'), may hold values from -6 to 6
- time_index: int32 [8], P('fsdp'), may hold values from 0 to 63
- ada_table: float32 [64, 2, 1536], replicated, may hold values from -3 to 3
- w_temporal: bfloat16 [1536, 4608], P('seq', 'fsdp'), may hold values from -0.15625 to 0.15625
Outputs:
- temporal_out: bfloat16 [8, 64, 128, 1536], P('fsdp', 'seq')
Inputs may be any that keep to these rules, and one draw needn't show every extreme that they name: `q_s`: real-valued entries. `k_s`: real-valued entries.
All inputs are finite; a program needn't handle non-finite values.
Results may differ from a plain program's by a relative error of at most 0.015.
Values may be sent and summed in bfloat16 or wider, within the bound.
No kernel may reach another device: no remote copies, remote signals or barrier semaphores. Data moves between devices by JAX's collectives and lax.ppermute only.
A program may use at most 64 MiB of HBM per device.

v0:
```python
import jax
import jax.numpy as jnp
from jax import lax
from jax.sharding import PartitionSpec as P

HEADS = 12
HEAD_SIZE = 128
ITERS = 3
relax_power = 0.8
norm_eps = 1e-06


def balanced_transport(logit_scores):
    potential_col = jnp.zeros_like(logit_scores[..., :1, :])
    potential_row = jnp.zeros_like(logit_scores[..., :, :1])
    for turn in range(ITERS):
        potential_row = -relax_power * jax.nn.logsumexp(
            logit_scores + potential_col, axis=-1, keepdims=True
        )
        potential_col = -relax_power * jax.nn.logsumexp(
            logit_scores + potential_row, axis=-2, keepdims=True
        )
    return jnp.exp(logit_scores + potential_row + potential_col).astype(jnp.bfloat16)


def temporal_attend(triple, logit_scale):
    temporal_logits = (
        jnp.einsum(
            "vfphd,vgphd->vphfg",
            triple[:, :, :, 0],
            triple[:, :, :, 1],
            preferred_element_type=jnp.float32,
        )
        * logit_scale
    )
    temporal_transport = balanced_transport(temporal_logits)
    temporal = jnp.einsum(
        "vphfg,vgphd->vfphd",
        temporal_transport,
        triple[:, :, :, 2],
        preferred_element_type=jnp.float32,
    )
    return temporal.astype(jnp.bfloat16)


def project(tokens, w_temporal):
    gathered = lax.all_gather(w_temporal, "fsdp", axis=1, tiled=True)
    whole = lax.all_gather(gathered, "seq", axis=0, tiled=True)
    return jnp.dot(tokens, whole, preferred_element_type=jnp.float32).astype(jnp.bfloat16)


def local(q_s, k_s, v_s, time_index, ada_table, w_temporal):
    positions = q_s.shape[2]
    width = HEADS * HEAD_SIZE
    logit_scale = 1.0 / HEAD_SIZE**0.5
    query_rows = q_s[0, 0].reshape(positions, HEADS, HEAD_SIZE)
    key_rows = k_s[0, 0].reshape(positions, HEADS, HEAD_SIZE)
    value_rows = v_s[0, 0].reshape(positions, HEADS, HEAD_SIZE)
    logit_scores = (
        jnp.einsum("pgl,bgl->gpb", query_rows, key_rows, preferred_element_type=jnp.float32)
        * logit_scale
    )
    transport_plan = balanced_transport(logit_scores)
    spatial_result = jnp.einsum(
        "bzg,gbq->zbq", transport_plan, value_rows, preferred_element_type=jnp.float32
    )
    spatial_result = spatial_result.reshape(positions, width).astype(jnp.bfloat16)
    selector = (jnp.arange(ada_table.shape[0]) == time_index[0]).astype(jnp.float32)
    modulate = jnp.einsum("t,tcw->cw", selector, ada_table, precision=lax.Precision.HIGHEST)
    hidden = spatial_result.astype(jnp.float32)
    scaled = hidden * lax.rsqrt(jnp.mean(hidden * hidden, axis=-1, keepdims=True) + norm_eps)
    modulated = (scaled * (1.0 + modulate[0]) + modulate[1]).astype(jnp.bfloat16)
    relayed = lax.all_to_all(modulated[None], "seq", split_axis=1, concat_axis=0, tiled=True)
    frames, local_pos = (relayed.shape[0], relayed.shape[1])
    triple = project(relayed.reshape(frames * local_pos, width), w_temporal)
    triple = triple.reshape(1, frames, local_pos, 3, HEADS, HEAD_SIZE)
    temporal = temporal_attend(triple, logit_scale).reshape(frames, local_pos, width)
    returned = lax.all_to_all(temporal, "seq", split_axis=0, concat_axis=1, tiled=True)
    return returned[None]


def solution(mesh):
    in_specs = (
        P("fsdp", "seq", None, None),
        P("fsdp", "seq", None, None),
        P("fsdp", "seq", None, None),
        P("fsdp"),
        P(),
        P("seq", "fsdp"),
    )
    out_specs = P("fsdp", "seq", None, None)
    return jax.shard_map(local, mesh=mesh, in_specs=in_specs, out_specs=out_specs, check_vma=False)
```

profile of v0, /device:TPU:1, one launch (start us, length us, event | category | flops | bytes accessed | tf_op | source)
XLA Modules:
  0.0 256.5 jit_solution(9671927672942869763)
XLA Ops:
  6.5 30.9 %all-gather = bf16[8,576,24]{1,2,0:T(8,128)(2,1)S(1)} all-gather(bf16[1,576,24]{1,2,0:T(8,128)(2,1)} %bitcast.56), channel_id=1, replica_groups=mesh['seq'=64,'fsdp'=8] {'fsdp'}, dimensions={0}, use_global_device_ids=true | all-gather | bytes 248832 | tf_op jit(solution)/shard_map/all_gather | solution.py:47
  37.5 0.9 reshape.479
  38.4 1.2 copy.71
  40.1 0.5 fusion.16
  40.6 0.5 exponential_reduce_fusion.11
  41.5 0.3 exponential_reduce_fusion.10
  42.1 0.5 exponential_reduce_fusion.9
  42.9 0.3 exponential_reduce_fusion.8
  43.5 0.5 exponential_reduce_fusion.7
  44.4 0.3 exponential_reduce_fusion.6
  44.7 0.5 multiply_reduce_fusion
  46.1 0.4 fusion.2
  46.7 0.6 copy.113
  47.3 0.5 broadcast.318
  47.9 3.0 %reduce.30 = bf16[128,1536]{1,0:T(8,128)(2,1)S(1)} reduce(bf16[128,1,1536]{2,1,0:T(2,128)(2,1)S(1)} %bitcast.49, bf16[]{:T(256)} %broadcast.318), dimensions={1}, to_apply=%bitcast.46.reduce_sub_computation | reduce | bytes 786434
  51.0 54.3 %all_to_all.8 = bf16[64,2,1536]{2,1,0:T(2,128)(2,1)S(1)} all-to-all(bf16[64,2,1536]{2,1,0:T(2,128)(2,1)S(1)} %reshape.485), channel_id=1, replica_groups=mesh['seq'=64,'fsdp'=8] {'seq'}, dimensions={0} | all-to-all | bytes 786432 | tf_op jit(solution)/shard_map/all_to_all | solution.py:73
  105.3 0.3 reshape.486
  105.7 93.0 %all-gather.3.cloned.1.call-done = bf16[1536,4608]{1,0:T(8,128)(2,1)} async-done(((bf16[24,4608]{1,0:T(8,128)(2,1)}), bf16[1536,4608]{1,0:T(8,128)(2,1)}) %all-gather.3.cloned.1.call-update) | async-done | bytes 14155792 | tf_op jit(solution)/shard_map/all_gather | solution.py:48
  198.7 7.0 %convolution_convert_fusion = bf16[128,4608]{1,0:T(8,128)(2,1)S(1)} fusion(bf16[1536,4608]{1,0:T(8,128)(2,1)} %all-gather.3.cloned.1.call-done, bf16[1,128,1536]{2,0,1:T(2,128)(2,1)S(1)} %bitcast.50), kind=kOutput, calls=%fused_computation | convolution fusion | flops 1812529152 | bytes 15728640 | tf_op jit(solution)/shard_map/dot_general | solution.py:49
  205.7 0.9 reshape.472
  206.9 0.5 fusion.17
  207.3 0.5 exponential_reduce_fusion.5
  207.9 0.3 add_reduce_fusion.3
  208.2 0.3 exponential_reduce_fusion.4
  208.8 0.5 exponential_reduce_fusion.3
  209.4 0.3 add_reduce_fusion.1
  209.7 0.3 exponential_reduce_fusion.2
  210.3 0.5 exponential_reduce_fusion.1
  211.1 0.3 exponential_reduce_fusion
  211.5 0.4 fusion.1
  212.4 36.4 %all_to_all.9 = bf16[64,2,1536]{2,1,0:T(2,128)(2,1)S(1)} all-to-all(bf16[64,2,1536]{2,1,0:T(2,128)(2,1)S(1)} %reshape.482), channel_id=1, replica_groups=mesh['seq'=64,'fsdp'=8] {'seq'}, dimensions={0} | all-to-all | bytes 786432 | tf_op jit(solution)/shard_map/all_to_all | solution.py:78
  248.8 0.9 broadcast_in_dim.2
  (52 shorter events, 4.2 us)
Async XLA Ops:
  6.5 39.5 %copy-start = (f32[64,2,1536]{2,1,0:T(2,128)S(1)}, f32[64,2,1536]{2,1,0:T(2,128)}, u32[]{:S(2)}) copy-start(f32[64,2,1536]{2,1,0:T(2,128)} %param.10) | copy-start | bytes 2359300
  6.5 33.1 %copy-start.1 = (bf16[1,1,128,1536]{3,2,1,0:T(8,128)(2,1)S(1)}, bf16[1,1,128,1536]{3,2,1,0:T(8,128)(2,1)}, u32[]{:S(2)}) copy-start(bf16[1,1,128,1536]{3,2,1,0:T(8,128)(2,1)} %param.7) | copy-start | bytes 1179652
  6.5 33.3 %copy-start.2 = (bf16[1,1,128,1536]{3,2,1,0:T(8,128)(2,1)S(1)}, bf16[1,1,128,1536]{3,2,1,0:T(8,128)(2,1)}, u32[]{:S(2)}) copy-start(bf16[1,1,128,1536]{3,2,1,0:T(8,128)(2,1)} %param.8) | copy-start | bytes 1179652
  6.5 192.1 %all-gather.3.cloned.1.call-start = ((), (), s32[]{:S(2)}) async-start(), calls=%async_computation.2 | async-start | bytes 14376960 | tf_op jit(solution)/shard_map/all_gather | solution.py:48
Sparse Core Ops, SparseCore 0:
  38.5 160.0 all-gather.2
where the time goes:
time: 257 us
  blocking collectives  122 us (47%)
  waiting for transfers between devices  93 us (36%)
  between operations  14.5 us (6%)
  other arithmetic  11 us (4%)
  matrix products  9.32 us (4%)
  local copies, waits for them, and re-layouts  6.94 us (3%)
    all_gather x1, waiting for transfers between devices, project(): whole = lax.all_gather(gathered, 'seq', axis=0, tiled=True)  93 us
    all_to_all x1, blocking collectives, local(): lax.all_to_all(modulated[None], 'seq', split_axis=1, concat_axis=0, tiled...  54.3 us
    all_to_all x1, blocking collectives, local(): lax.all_to_all(temporal, 'seq', split_axis=0, concat_axis=1, tiled=True)  36.4 us
    all_gather x1, blocking collectives, project(): gathered = lax.all_gather(w_temporal, 'fsdp', axis=1, tiled=True)  30.9 us
    dot_general x1, matrix products, project(): jnp.dot(tokens, whole, preferred_element_type=jnp.float32)  7.04 us
  transfers between devices with their start and end apart: 1, of which 1 were waited for; matrix products, arithmetic and copies ran while one was open for 5% of the time, Pallas kernels for 0%

commit v1 on v0

--- a/solution.py
+++ b/solution.py
@@ -45,7 +45,9 @@
 
 def project(tokens, w_temporal):
     gathered = lax.all_gather(w_temporal, "fsdp", axis=1, tiled=True)
-    whole = lax.all_gather(gathered, "seq", axis=0, tiled=True)
+    whole = jnp.concatenate(
+        lax.all_to_all(jnp.stack([gathered] * lax.axis_size("seq")), "seq", 0, 0), axis=0
+    )
     return jnp.dot(tokens, whole, preferred_element_type=jnp.float32).astype(jnp.bfloat16)
 
 

time: 257 us -> 753 us (2.93)
  waiting for transfers between devices: 93 us -> 608 us
  blocking collectives: 122 us -> 72 us
  starting transfers between devices: 0.01 us -> 36 us
  between operations: 14.5 us -> 1.17 us
  local copies, waits for them, and re-layouts: 6.94 us -> 15.1 us
    all_to_all x0 -> x2, waiting for transfers between devices: none -> 608 us  [the longest x1 608 us: project(): lax.all_to_all(jnp.stack([gathered] * lax.axis_size('seq')), 'seq', 0, 0)]
    all_gather x1 -> x0, waiting for transfers between devices: 93 us -> none  [project(): whole = lax.all_gather(gathered, 'seq', axis=0, tiled=True)]
    all_to_all x1 -> x0, blocking collectives: 54.3 us -> none  [local(): lax.all_to_all(modulated[None], 'seq', split_axis=1, concat_axis=0, tiled...]
    all_to_all x0 -> x2, starting transfers between devices: none -> 36 us  [the longest x1 18.1 us: local(): lax.all_to_all(modulated[None], 'seq', split_axis=1, concat_axis=0, tiled...]
  transfers between devices with their start and end apart: 1 -> 2, of which waited for: 1 -> 1; matrix products, arithmetic and copies ran while one was open for 5% -> 0% of each run, Pallas kernels for 0% -> 0%
where the time goes in v1:
time: 753 us
  waiting for transfers between devices  608 us (81%)
  blocking collectives  72 us (10%)
  starting transfers between devices  36 us (5%)
  local copies, waits for them, and re-layouts  15.1 us (2%)
  other arithmetic  11.1 us (1%)
  matrix products  9.32 us (1%)
    all_to_all x1, waiting for transfers between devices, project(): lax.all_to_all(jnp.stack([gathered] * lax.axis_size('seq')), 'seq', 0, 0)  608 us
    all_to_all x1, blocking collectives, local(): lax.all_to_all(temporal, 'seq', split_axis=0, concat_axis=1, tiled=True)  41 us
    all_gather x1, blocking collectives, project(): gathered = lax.all_gather(w_temporal, 'fsdp', axis=1, tiled=True)  31 us
    all_to_all x1, starting transfers between devices, local(): lax.all_to_all(modulated[None], 'seq', split_axis=1, concat_axis=0, tiled...  18.1 us
    all_to_all x1, starting transfers between devices, project(): lax.all_to_all(jnp.stack([gathered] * lax.axis_size('seq')), 'seq', 0, 0)  17.9 us
  transfers between devices with their start and end apart: 2, of which 1 were waited for; matrix products, arithmetic and copies ran while one was open for 0% of the time, Pallas kernels for 0%

profile of v1, /device:TPU:1, one launch (start us, length us, event | category | flops | bytes accessed | tf_op | source)
XLA Modules:
  0.0 752.6 jit_solution(17460975694439020911)
XLA Ops:
  0.0 1.3 copy.76
  1.3 1.2 copy.72
  2.5 1.2 copy.73
  3.7 0.5 fusion.16
  4.2 0.5 exponential_reduce_fusion.11
  5.1 0.3 exponential_reduce_fusion.10
  5.7 0.5 exponential_reduce_fusion.9
  7.1 0.5 exponential_reduce_fusion.7
  8.3 0.5 multiply_reduce_fusion
  9.7 0.4 fusion.2
  10.4 0.6 copy.114
  11.0 0.5 broadcast.320
  11.5 3.0 reduce.30
  14.5 0.9 reshape.491
  15.4 18.1 %all-to-all-start = ((bf16[64,2,1536]{2,1,0:T(2,128)(2,1)}), bf16[64,2,1536]{2,1,0:T(2,128)(2,1)S(1)}, u32[]{:S(2)}, u32[]{:S(2)}) async-start(bf16[64,2,1536]{2,1,0:T(2,128)(2,1)} %reshape.491), calls=%async_computation | async-start | bytes 786432 | tf_op jit(solution)/shard_map/all_to_all | solution.py:75
  33.5 31.0 %all-gather = bf16[8,576,24]{1,2,0:T(8,128)(2,1)S(1)} all-gather(bf16[1,576,24]{1,2,0:T(8,128)(2,1)S(1)} %bitcast.57), channel_id=1, replica_groups=mesh['seq'=64,'fsdp'=8] {'fsdp'}, dimensions={0}, use_global_device_ids=true | all-gather | bytes 248832 | tf_op jit(solution)/shard_map/all_gather | solution.py:47
  64.7 6.0 stack.2
  70.8 17.9 %all-to-all-start.1 = ((bf16[64,24,4608]{2,1,0:T(8,128)(2,1)}), bf16[64,24,4608]{2,1,0:T(8,128)(2,1)}, u32[]{:S(2)}, u32[]{:S(2)}) async-start(bf16[64,24,4608]{2,1,0:T(8,128)(2,1)} %stack.2), calls=%async_computation.1 | async-start | bytes 28311552 | tf_op jit(solution)/shard_map/all_to_all | solution.py:49
  88.7 0.3 reshape.492
  89.0 607.9 %all-to-all-done.1 = bf16[64,24,4608]{2,1,0:T(8,128)(2,1)} async-done(((bf16[64,24,4608]{2,1,0:T(8,128)(2,1)}), bf16[64,24,4608]{2,1,0:T(8,128)(2,1)}, u32[]{:S(2)}, u32[]{:S(2)}) %all-to-all-start.1) | async-done | bytes 14155808 | tf_op jit(solution)/shard_map/all_to_all | solution.py:49
  697.0 7.0 convolution_convert_fusion
  704.0 0.9 reshape.478
  705.2 0.5 fusion.17
  705.6 0.5 exponential_reduce_fusion.5
  706.5 0.3 exponential_reduce_fusion.4
  707.1 0.5 exponential_reduce_fusion.3
  708.0 0.3 exponential_reduce_fusion.2
  708.6 0.5 exponential_reduce_fusion.1
  709.4 0.3 exponential_reduce_fusion
  709.8 0.4 fusion.1
  710.7 41.0 %all_to_all.23 = bf16[64,2,1536]{2,1,0:T(2,128)(2,1)S(1)} all-to-all(bf16[64,2,1536]{2,1,0:T(2,128)(2,1)S(1)} %reshape.488), channel_id=1, replica_groups=mesh['seq'=64,'fsdp'=8] {'seq'}, dimensions={0} | all-to-all | bytes 786432 | tf_op jit(solution)/shard_map/all_to_all | solution.py:80
  751.7 0.9 broadcast_in_dim.2
  (51 shorter events, 5.0 us)
Async XLA Ops:
  0.0 9.7 %copy-start = (f32[64,2,1536]{2,1,0:T(2,128)S(1)}, f32[64,2,1536]{2,1,0:T(2,128)}, u32[]{:S(2)}) copy-start(f32[64,2,1536]{2,1,0:T(2,128)} %param.10) | copy-start | bytes 2359300
  0.0 33.5 %copy-start.1 = (bf16[24,576]{1,0:T(8,128)(2,1)S(1)}, bf16[24,576]{1,0:T(8,128)(2,1)}, u32[]{:S(2)}) copy-start(bf16[24,576]{1,0:T(8,128)(2,1)} %param.11) | copy-start | bytes 82948
  15.4 49.3 %all-to-all-start = ((bf16[64,2,1536]{2,1,0:T(2,128)(2,1)}), bf16[64,2,1536]{2,1,0:T(2,128)(2,1)S(1)}, u32[]{:S(2)}, u32[]{:S(2)}) async-start(bf16[64,2,1536]{2,1,0:T(2,128)(2,1)} %reshape.491), calls=%async_computation | async-start | bytes 786432 | tf_op jit(solution)/shard_map/all_to_all | solution.py:75
  70.8 626.2 %all-to-all-start.1 = ((bf16[64,24,4608]{2,1,0:T(8,128)(2,1)}), bf16[64,24,4608]{2,1,0:T(8,128)(2,1)}, u32[]{:S(2)}, u32[]{:S(2)}) async-start(bf16[64,24,4608]{2,1,0:T(8,128)(2,1)} %stack.2), calls=%async_computation.1 | async-start | bytes 28311552 | tf_op jit(solution)/shard_map/all_to_all | solution.py:49
